TPU v7x, 32 devices: a whole 2x2x4 slice. The times are simulated.
32 devices in a mesh: rows: 8 (over z, x), scales: 4 (over y, core).
Axes of the slice: x: 2, y: 2, z: 4, core: 2. Of those that a mesh axis runs over, the one named last changes fastest.
Arguments:
- image_now: float32 [256, 8192], P(('rows', 'scales')), may hold values from 0.1 to 4
- gradient: float32 [256, 8192], P(('rows', 'scales')), may hold values from -140 to 140
- hessian_weight: float32 [256, 8192], P(('rows', 'scales')), may hold values from 0.1 to 10
- psf_tiles: float32 [32, 256], P(('rows', 'scales')), may hold values from -0.5 to 1.7
- facet_of_row: int32 [256], P(('rows', 'scales')), may hold values from 0 to 31, never falling along the last dimension, each value on 1 to 32 neighbouring positions
- tile_slot: int32 [32], replicated, may hold values from 0 to 31, each once
- thresholds: float32 [4], replicated, may hold values from 0.2 to 2
Outputs:
- new_image: float32 [256, 8192], P(('rows', 'scales'))
Inputs may be any that keep to these rules, and one draw needn't show every extreme that they name: `facet_of_row`: facet numbers never fall along the rows; every facet covers 1 to 32 rows, and some facet exactly 32. `tile_slot`: each facet's tile stands in a different row of psf_tiles, and every row holds one.
All inputs are finite; a program needn't handle non-finite values.
Results may differ from a plain program's by a relative error of at most 0.0001.
Values sent between devices are 32-bit elements; how exact they have to be, the bound alone decides.
A program may use at most 64 MiB of HBM per device.

v0:
```python
import functools

import jax
import jax.numpy as jnp
import numpy as np
from jax import lax
from jax.experimental import pallas as pl
from jax.experimental.pallas import tpu as pltpu
from jax.sharding import PartitionSpec as P

TILE = 16
HALF = TILE // 2
SUBITERS = 2
LANES = 128
BLOCK = 32
GROUPS = LANES // BLOCK
WIDTH = 8 * BLOCK
AXES = ("rows", "scales")
VMEM = pl.BlockSpec(memory_space=pltpu.VMEM)


def spline_matrices(levels):
    w = np.arange(WIDTH)
    same = (w[:, None] // BLOCK) == (w[None, :] // BLOCK)
    place = w % BLOCK
    nearer = place + np.where(place < BLOCK // 2, BLOCK, -BLOCK)
    planes = []
    for level in range(levels):
        d = 2**level
        for column in (place, nearer):
            o = np.abs(column[:, None] - place[None, :])
            coef = np.where(o == 0, 0.375, np.where(o == d, 0.25, np.where(o == 2 * d, 0.0625, 0.0)))
            planes.append(np.where(same, coef, 0.0))
    return jnp.asarray(np.stack(planes), jnp.bfloat16)


def halves(x):
    high = x.astype(jnp.bfloat16)
    low = (x - high.astype(jnp.float32)).astype(jnp.bfloat16)
    return high, low


def dot(a, b):
    return jnp.dot(a, b, preferred_element_type=jnp.float32)


def block_shift(x, s):
    if s == 0:
        return x
    count = x.shape[0] // GROUPS
    parts = [x[p * count : (p + 1) * count] for p in range(GROUPS)]
    row = lax.broadcasted_iota(jnp.int32, parts[0].shape, 0)
    if s == 1:
        last = jnp.where(row == count - 1, 0.0, pltpu.roll(parts[0], count - 1, 0))
        return jnp.concatenate(parts[1:] + [last], axis=0)
    first = jnp.where(row == 0, 0.0, pltpu.roll(parts[-1], 1, 0))
    return jnp.concatenate([first] + parts[:-1], axis=0)


def beside(x):
    lane = lax.broadcasted_iota(jnp.int32, x.shape, 1) % BLOCK
    return jnp.where(lane < BLOCK // 2, block_shift(x, 1), block_shift(x, -1))


def blur(stripes, high_ref, low_ref):
    total = None
    for t, x in enumerate(stripes):
        for n, y in enumerate((x, beside(x))):
            high, low = halves(y)
            w = high_ref[t * 2 + n]
            part = dot(high, w) + dot(low, w) + dot(high, low_ref[t * 2 + n])
            total = part if total is None else total + part
    return total


def to_blocks(src_ref, dst_ref, tiles):
    count = src_ref.shape[1] // LANES
    for q in range(count):
        tiles[pl.ds(8 * q, 8), :] = src_ref[:, q * LANES : (q + 1) * LANES]
    group = lax.broadcasted_iota(jnp.int32, (count, LANES), 1) // BLOCK
    for half in range(2):
        outs = [None] * GROUPS
        for k in range(4):
            a = tiles[pl.ds(half * 4 + k, count, stride=8), :]
            for p in range(GROUPS):
                shift = BLOCK * ((k - p) % 4)
                moved = pltpu.roll(a, shift, 1) if shift else a
                outs[p] = moved if k == 0 else jnp.where(group == k, moved, outs[p])
        for p in range(GROUPS):
            dst_ref[p * count : (p + 1) * count, half * LANES : (half + 1) * LANES] = outs[p]


def from_blocks(src_ref, dst_ref, tiles):
    count = dst_ref.shape[1] // LANES
    group = lax.broadcasted_iota(jnp.int32, (count, LANES), 1) // BLOCK
    for half in range(2):
        for k in range(4):
            out = None
            for p in range(GROUPS):
                x = src_ref[p * count : (p + 1) * count, half * LANES : (half + 1) * LANES]
                shift = BLOCK * ((p - k) % 4)
                moved = pltpu.roll(x, shift, 1) if shift else x
                out = moved if p == 0 else jnp.where(group == p, moved, out)
            tiles[pl.ds(half * 4 + k, count, stride=8), :] = out
    for q in range(count):
        dst_ref[:, q * LANES : (q + 1) * LANES] = tiles[pl.ds(8 * q, 8), :]


def build_weights(base_ref, lead, high_ref, low_ref, wide):
    lane = lax.broadcasted_iota(jnp.int32, (8, WIDTH), 1) % BLOCK
    for t in range(3):
        base = base_ref[8 * t : 8 * t + 8, :]
        for w in range(BLOCK):
            for n, s in enumerate((0, 1 if w < BLOCK // 2 else -1)):
                moved = pltpu.roll(base, (w - lead + BLOCK * s) % WIDTH, 1)
                x = lane - (w - lead + BLOCK * s)
                kept = jnp.where((x >= 0) & (x < TILE), moved, 0.0)
                for half in range(2):
                    wide[n, half, pl.ds(w, 8, stride=BLOCK), :] = kept[
                        :, half * LANES : (half + 1) * LANES
                    ]
        for n in range(2):
            for half in range(2):
                high, low = halves(wide[n, half])
                high_ref[t * 2 + n, :, half * LANES : (half + 1) * LANES] = high
                low_ref[t * 2 + n, :, half * LANES : (half + 1) * LANES] = low


def moved_rows(vregs, rolls, i, d):
    if d % 4 == 0:
        return vregs[i + d // 4]
    shift = (-BLOCK * d) % LANES

    def rolled(n):
        if (n, shift) not in rolls:
            rolls[(n, shift)] = pltpu.roll(vregs[n], shift, 1)
        return rolls[(n, shift)]

    lane = lax.broadcasted_iota(jnp.int32, vregs[i].shape, 1)
    if d > 0:
        return jnp.where(lane < LANES - BLOCK * d, rolled(i), rolled(i + 1))
    return jnp.where(lane >= -BLOCK * d, rolled(i), rolled(i - 1))


def column_cascade(stripe_refs, alive, levels_ref, step_rows):
    reach = len(stripe_refs) // 2
    levels = levels_ref.shape[0]

    def chunk(n, carry):
        rows = pl.ds(pl.multiple_of(n * step_rows, step_rows), step_rows)
        vregs = {}
        for t, ref in enumerate(stripe_refs):
            for half in range(2):
                vregs[2 * t + half] = ref[rows, half * LANES : (half + 1) * LANES]
        own = 2 * reach
        for level in range(levels):
            d = 2**level
            left = 2 ** (levels + 1) - 2 ** (level + 2)
            margin = -(-left // 4)
            rolls, out = {}, {}
            keys = vregs
            for i in range(own - margin, own + 2 + margin):
                outer = moved_rows(keys, rolls, i, -2 * d) + moved_rows(keys, rolls, i, 2 * d)
                inner = moved_rows(keys, rolls, i, -d) + moved_rows(keys, rolls, i, d)
                value = 0.0625 * outer + 0.25 * inner + 0.375 * keys[i]
                t = i // 2
                out[i] = value if t == reach else value * alive[t]
            vregs = out
            for half in range(2):
                levels_ref[level, rows, half * LANES : (half + 1) * LANES] = out[own + half]
        return carry

    lax.fori_loop(0, stripe_refs[0].shape[0] // step_rows, chunk, 0)


def row_cascade(levels_ref, spline_ref):
    levels = levels_ref.shape[0]
    for level in range(levels):

        def one(k, carry):
            x = levels_ref[k]
            total = None
            for n, y in enumerate((x, beside(x))):
                high, low = halves(y)
                w = spline_ref[level * 2 + n]
                part = dot(high, w) + dot(low, w)
                total = part if total is None else total + part
            levels_ref[k] = total
            return carry

        lax.fori_loop(level, levels, one, 0)


def keep(own, levels_ref, limits):
    levels = levels_ref.shape[0]
    smooth = own
    total = None
    for k in range(levels):
        smoother = levels_ref[k]
        detail = smooth - smoother
        part = detail - jnp.clip(detail, -limits[k], limits[k])
        total = part if total is None else total + part
        smooth = smoother
    return total + smooth


def build_bases(taps, flipped, forward, adjoint):
    lane = lax.broadcasted_iota(jnp.int32, (8, WIDTH), 1)
    sub = lax.broadcasted_iota(jnp.int32, (8, WIDTH), 0)
    group, inside = lane // BLOCK, lane % BLOCK < TILE
    own = flipped[...]
    turned = [pltpu.roll(own, TILE * n, 1) if n else own for n in range(TILE)]
    forward[...] = jnp.zeros_like(forward)
    for a in range(TILE):
        placed = jnp.zeros((8, WIDTH), jnp.float32)
        for r in range(8):
            placed = jnp.where((sub == r) & (group == r) & inside, turned[(2 * r - a) % TILE], placed)
        forward[a : a + 8, :] += placed
    for t in range(3):
        x = taps[t]
        row = sub + 8 * t
        tap = group - row + TILE
        placed = jnp.zeros((8, WIDTH), jnp.float32)
        for n in range(TILE):
            moved = pltpu.roll(x, TILE * n, 1) if n else x
            use = ((group + row) % TILE == n) & inside & (tap >= 0) & (tap < TILE)
            placed = jnp.where(use, moved, placed)
        adjoint[8 * t : 8 * t + 8, :] = placed


def kernel(
    count, scales, side,
    image, gradient, weight, psf, facet, slot_of, thresholds, spline,
    out,
    xi, xg, xh, current, near, middle, far, psf_all, taps, flipped, base_f, base_a, fh, fl, ah, al,
    levels, sums, tiles, wide,
    psf_send, psf_recv, sum_send, sum_recv, tap_send, tap_recv, near_send, near_recv, far_send, far_recv,
):
    me = lax.axis_index("rows") * scales + lax.axis_index("scales")
    barrier = pltpu.get_barrier_semaphore()

    def device(index):
        return (index // scales, index % scales)

    def peer(k):
        return (me + k) % count

    def exists(o):
        return (me + o >= 0) & (me + o < count)

    def greet(k, carry):
        pl.semaphore_signal(barrier, inc=1, device_id=device(peer(k)), device_id_type=MESH)
        return carry

    lax.fori_loop(1, count, greet, 0)

    def copy(src, dst, send_sem, recv_sem, index):
        return pltpu.make_async_remote_copy(
            src_ref=src, dst_ref=dst, send_sem=send_sem, recv_sem=recv_sem,
            device_id=device(index), device_id_type=MESH,
        )

    def share(src, pool, send, recv):
        def start(k, carry):
            copy(src, pool.at[me], send.at[k], recv.at[me], peer(k)).start()
            return carry

        lax.fori_loop(1, count, start, 0)

    def collect(src, pool, send, recv):
        def wait(k, carry):
            copy(src, pool.at[peer(k)], send.at[k], recv.at[peer(k)], peer(k)).wait()
            return carry

        lax.fori_loop(1, count, wait, 0)

    def spread(src, place, send, recv, offsets):
        for o in offsets:

            @pl.when(exists(o))
            def _():
                copy(src, place(-o), send(o), recv(-o), me + o).start()

    def arrive(src, place, send, recv, offsets):
        for o in offsets:

            @pl.when(exists(o))
            def _():
                copy(src, place(o), send(o), recv(o), me + o).wait()

    def near_spread(e, src):
        args = (src, lambda o: near.at[e, (o + 1) // 2], lambda o: near_send.at[e, (o + 1) // 2],
                lambda o: near_recv.at[e, (o + 1) // 2], (-1, 1))
        spread(*args)
        return lambda: arrive(*args)

    offsets = [sign * o for o in range(1, side + 1) for sign in (-1, 1)]

    evens = [0] + [o for o in offsets if o % 2 == 0]
    odds = [o for o in offsets if o % 2]
    delta = 1 - 2 * (me % 2)

    def direct(e, o):
        return copy(far.at[side], far.at[side - o], far_send.at[e, side + o], far_recv.at[e, side - o], me + o)

    def arrival(e, o):
        return copy(far.at[side], far.at[side + o], far_send.at[e, side + o], far_recv.at[e, side + o], me + o)

    def passed(e, o):
        place = o - delta + side
        return copy(far.at[side + o], far.at[place], far_send.at[e, place], far_recv.at[e, place], me + delta)

    def passes(o):
        return exists(o) & (o - delta >= -side) & (o - delta <= side)

    def far_exchange(e):
        for o in evens[1:]:

            @pl.when(exists(o))
            def _():
                direct(e, o).start()

        for o in evens:
            if o:

                @pl.when(exists(o))
                def _():
                    arrival(e, o).wait_recv()

            @pl.when(passes(o))
            def _():
                passed(e, o).start()

        for o in odds:

            @pl.when(exists(o))
            def _():
                arrival(e, o).wait_recv()

        for o in evens:
            if o:

                @pl.when(exists(o))
                def _():
                    direct(e, o).wait_send()

            @pl.when(passes(o))
            def _():
                passed(e, o).wait_send()

    to_blocks(gradient, xg, tiles)
    for o in (-1, 1):

        @pl.when(jnp.logical_not(exists(o)))
        def _():
            for e in range(near.shape[0]):
                near[e, (o + 1) // 2] = jnp.zeros(near.shape[2:], jnp.float32)
            taps[o + 1] = jnp.zeros(taps.shape[1:], jnp.float32)

    for o in offsets:

        @pl.when(jnp.logical_not(exists(o)))
        def _():
            far[o + side] = jnp.zeros(far.shape[1:], jnp.float32)

    pl.semaphore_wait(barrier, count - 1)
    share(psf, psf_all, psf_send, psf_recv)
    near_done = near_spread(0, xg)
    to_blocks(image, xi, tiles)
    to_blocks(weight, xh, tiles)
    psf_all[me] = psf[...]
    collect(psf, psf_all, psf_send, psf_recv)
    for r in range(8):
        both = psf_all[slot_of[facet[r]]]
        taps[1, r : r + 1, :] = both[0:1]
        flipped[r : r + 1, :] = both[1:2]
    tap_args = (taps.at[1], lambda o: taps.at[o + 1], lambda o: tap_send.at[(o + 1) // 2],
                lambda o: tap_recv.at[(o + 1) // 2], (-1, 1))
    spread(*tap_args)
    arrive(*tap_args)
    build_bases(taps, flipped, base_f, base_a)
    build_weights(base_f, HALF - 1, fh, fl, wide)
    alive = [None if t == side else jnp.where(exists(t - side), 1.0, 0.0) for t in range(2 * side + 1)]

    for sweep in range(SUBITERS):
        if sweep == 0:
            descent = xg
        else:
            descent = middle
            e = 3 * sweep - 2
            done = near_spread(e, current_change)
            done()
            change = current_change[...]
            pushed = xh[...] * blur([near[e, 0], change, near[e, 1]], fh, fl)
            far[side] = pushed
            near_done = near_spread(e + 1, far.at[side])
            near_done()
            middle[...] = xg[...] + blur([near[e + 1, 0], pushed, near[e + 1, 1]], ah, al)
            near_done = near_spread(e + 2, middle)
        near_done()
        e = 3 * sweep
        d = descent[...]
        b = blur([near[e, 0], d, near[e, 1]], fh, fl)

        def lanes(x):
            column = jnp.sum(x, axis=0, keepdims=True)
            return column[:, :LANES] + column[:, LANES:]

        sums[sweep, me] = jnp.concatenate([lanes(d * d), lanes(xh[...] * b * b)], axis=0)
        own = sums.at[sweep, me]
        share(own, sums.at[sweep], sum_send.at[sweep], sum_recv.at[sweep])
        if sweep == 0:
            build_weights(base_a, HALF, ah, al, wide)
        collect(own, sums.at[sweep], sum_send.at[sweep], sum_recv.at[sweep])
        totals = jnp.sum(jnp.sum(sums[sweep], axis=0), axis=1, keepdims=True)
        step = totals[0:1] / totals[1:2]
        start = xi if sweep == 0 else current
        far[side] = start[...] - step * d
        far_exchange(sweep)
        stripes = [far.at[t] for t in range(2 * side + 1)]
        column_cascade(stripes, alive, levels, 8)
        row_cascade(levels, spline)
        new = keep(far[side], levels, [step * thresholds[k] for k in range(levels.shape[0])])
        current[...] = new
        if sweep < SUBITERS - 1:
            current_change = far.at[side]
            current_change[...] = new - xi[...]
    from_blocks(current, out, tiles)


MESH = pl.DeviceIdType.MESH


def body(image_now, gradient, hessian_weight, psf_tiles, facet_of_row, tile_slot, thresholds):
    band, columns = image_now.shape
    levels = thresholds.shape[0]
    blocks = columns // BLOCK
    scales = lax.axis_size("scales")
    count = lax.axis_size("rows") * scales
    reach = 2 ** (levels + 1) - 2
    side = -(-reach // band)
    own = psf_tiles.reshape(TILE, TILE)
    psf = jnp.stack([own, jnp.flip(own, axis=1)]).reshape(2, TILE * TILE)
    plane = (blocks, WIDTH)
    table = pltpu.VMEM((6, WIDTH, WIDTH), jnp.bfloat16)
    f32 = lambda *shape: pltpu.VMEM(shape, jnp.float32)
    sem = lambda *shape: pltpu.SemaphoreType.DMA(shape)
    smem = pl.BlockSpec(memory_space=pltpu.SMEM)
    exchanges = 3 * SUBITERS - 2
    return pl.pallas_call(
        functools.partial(kernel, count, scales, side),
        out_shape=jax.ShapeDtypeStruct((band, columns), jnp.float32),
        in_specs=[VMEM] * 4 + [smem] * 3 + [VMEM],
        out_specs=VMEM,
        scratch_shapes=[
            f32(*plane), f32(*plane), f32(*plane), f32(*plane),
            f32(exchanges, 2, *plane), f32(*plane), f32(2 * side + 1, *plane),
            f32(count, 2, TILE * TILE), f32(3, 8, TILE * TILE), f32(8, TILE * TILE),
            f32(3 * band, WIDTH), f32(3 * band, WIDTH), table, table, table, table,
            f32(levels, *plane), f32(SUBITERS, count, 2, LANES),
            f32(columns // LANES * 8, LANES), f32(2, 2, WIDTH, LANES),
            sem(count), sem(count), sem(SUBITERS, count), sem(SUBITERS, count), sem(2), sem(2),
            sem(exchanges, 2), sem(exchanges, 2),
            sem(SUBITERS, 2 * side + 1), sem(SUBITERS, 2 * side + 1),
        ],
        compiler_params=pltpu.CompilerParams(
            collective_id=0, has_side_effects=True, vmem_limit_bytes=56 * 1024 * 1024
        ),
    )(image_now, gradient, hessian_weight, psf, facet_of_row, tile_slot, thresholds, spline_matrices(levels))


def solution(mesh):
    band = P(AXES, None)
    in_specs = (band, band, band, band, P(AXES), P(), P())
    return jax.shard_map(body, mesh=mesh, in_specs=in_specs, out_specs=band, check_vma=False)
```

profile of v0, /device:TPU:13, one launch (start us, length us, event | category | flops | bytes accessed | tf_op | source)
XLA Modules:
  0.0 121.5 jit_solution(11664759540007953708)
XLA Ops:
  0.0 0.0 copy-start
  0.0 0.5 broadcast.3
  0.5 0.2 copy-done
  0.7 0.7 reduce.3
  1.3 0.1 reshape.8
  1.4 0.1 rev.4
  1.5 0.1 stack.6
  1.6 0.6 pad_maximum_fusion.psf
  2.2 117.6 %shard_map.82 = f32[8,8192]{1,0:T(8,128)} custom-call(f32[8,8192]{1,0:T(8,128)} %image.1, f32[8,8192]{1,0:T(8,128)} %gradient.1, f32[8,8192]{1,0:T(8,128)} %weight.1, f32[2,256]{1,0:T(2,128)} %pad_maximum_fusion.psf, s32[8]{0:T(128)} %facet.1, s32[32]{0:T(128)} %slot_of.1, f32[4]{0:T(128)} %thresholds.1, bf16[8,256,256]{2,1,0:T(8,128)(2,1)} %constant.2.clone.spline), custom_call_target="tpu_custom_call" | custom-call | tf_op jit(solution)/shard_map/pallas_call | solution.py:450
  119.8 1.7 %copy.10 = f32[8,8192]{1,0:T(8,128)} copy(f32[8,8192]{1,0:T(8,128)} %shard_map.82) | data formatting | bytes 524288
Async XLA Ops:
  0.0 0.7 copy-start
where the time goes:
time: 122 us; the launch traced here: 121 us
  Pallas kernels  118 us (97%)
  local copies, waits for them, and re-layouts  2.59 us (2%)
  other arithmetic  1.26 us (1%)
    pallas_call x1, Pallas kernels, body(): pl.pallas_call(functools.partial(kernel, count, scales, side), out_shape=...  118 us

commit v1 on v0

v1 whole, which is shorter than its diff:
```python
import functools

import jax
import jax.numpy as jnp
from jax import lax
from jax.experimental import pallas as pl
from jax.experimental.pallas import tpu as pltpu
from jax.sharding import PartitionSpec as P

TILE = 16
HALF = TILE // 2
SUBITERS = 2
LANES = 128
SHIFTS = 4
AXES = ("rows", "scales")
MESH = pl.DeviceIdType.MESH
VMEM = pl.BlockSpec(memory_space=pltpu.VMEM)


def up8(n):
    return -(-n // 8) * 8


def halves(x):
    high = x.astype(jnp.bfloat16)
    low = (x - high.astype(jnp.float32)).astype(jnp.bfloat16)
    return high, low


def dot(a, b):
    return jnp.dot(a, b, preferred_element_type=jnp.float32)


def dot_t(a, b):
    return lax.dot_general(a, b, (((1,), (1,)), ((), ())), preferred_element_type=jnp.float32)


def over(low, high, size, body):
    count = (high - low) // size
    assert count * size == high - low

    def one(n, carry):
        body(pl.multiple_of(low + n * size, 8))
        return carry

    lax.fori_loop(0, count, one, 0)


def block(total, limit, step):
    for size in range(limit // step * step, 0, -step):
        if total % size == 0:
            return size


def kernel(
    count, scales, group, levels, margin,
    image, gradient, weight, psf, facet, slot_of, thresholds,
    out,
    land, psf_all, slots, tg, ti, th, cur, work, smooth, y, sh, sl, cc, sums, pack_up, pack_down, got_up, got_down, back,
    psf_send, psf_recv, slot_send, slot_recv, in_send, in_recv, fwd_send, fwd_recv,
    sum_send, sum_recv, halo_send, halo_recv, out_send, out_recv,
):
    me = lax.axis_index("rows") * scales + lax.axis_index("scales")
    team, place = me // group, me % group
    teams = count // group
    band = image.shape[0]
    columns = image.shape[1]
    own = columns // group
    mid = margin // band
    bands = LANES // band
    side = margin + (SUBITERS - 1) * (margin + TILE)
    off = side + margin
    has_up, has_down = team > 0, team < teams - 1
    first, last = place == 0, place == group - 1
    barrier = pltpu.get_barrier_semaphore()
    lane = lax.broadcasted_iota(jnp.int32, (1, LANES), 1)

    def device(index):
        return (index // scales, index % scales)

    def peer(k):
        return (me + k) % count

    def greet(k, carry):
        pl.semaphore_signal(barrier, inc=1, device_id=device(peer(k)), device_id_type=MESH)
        return carry

    lax.fori_loop(1, count, greet, 0)

    def copy(src, dst, send_sem, recv_sem, index):
        return pltpu.make_async_remote_copy(
            src_ref=src, dst_ref=dst, send_sem=send_sem, recv_sem=recv_sem,
            device_id=device(index), device_id_type=MESH,
        )

    def share(src, pool, send, recv):
        def start(k, carry):
            copy(src, pool.at[me], send.at[k], recv.at[me], peer(k)).start()
            return carry

        lax.fori_loop(1, count, start, 0)

    def collect(src, pool, send, recv):
        def wait(k, carry):
            copy(src, pool.at[peer(k)], send.at[k], recv.at[peer(k)], peer(k)).wait()
            return carry

        lax.fori_loop(1, count, wait, 0)

    def piece(e, j):
        src = (image, gradient, weight)[e]
        low, high = max(j * own - LANES, 0), min((j + 1) * own + LANES, columns)
        start = low - (j * own - LANES)
        return src.at[:, low:high], land.at[e, mid + place, :, start : start + high - low]

    def in_start(e):
        for j in range(group):
            src, dst = piece(e, j)

            @pl.when(place != j)
            def _():
                copy(src, dst, in_send.at[e, j], in_recv.at[e, place], team * group + j).start()

            @pl.when(place == j)
            def _():
                pltpu.make_async_copy(src, dst, in_recv.at[e, j]).start()

    def in_wait(e, k):
        for j, when in ((0, first), (group - 1, last), (1, jnp.logical_not(first | last))):
            low, high = max(j * own - LANES, 0), min((j + 1) * own + LANES, columns)
            start = low - (j * own - LANES)
            dst = land.at[e, mid + k, :, start : start + high - low]

            @pl.when(when)
            def _():
                copy(dst, dst, in_send.at[e, 0], in_recv.at[e, k], me).wait_recv()

    def in_done(e):
        for j in range(group):
            src, dst = piece(e, j)

            @pl.when(place != j)
            def _():
                copy(src, dst, in_send.at[e, j], in_recv.at[e, place], team * group + j).wait_send()

    def forward(e, k, reach):
        out_ = []
        if k < reach:
            out_.append((has_up, me - group, mid + group + k, mid - 1 - k))
        if k >= group - reach:
            out_.append((has_down, me + group, mid - group + k, mid + 2 * group - 1 - k))
        return out_

    def forward_start(e, k, reach):
        for when, index, there, _ in forward(e, k, reach):

            @pl.when(when)
            def _():
                copy(land.at[e, mid + k], land.at[e, there], fwd_send.at[e, there], fwd_recv.at[e, there], index).start()

    def forward_done(e, reach):
        for k in range(group):
            for when, index, there, _ in forward(e, k, reach):

                @pl.when(when)
                def _():
                    copy(land.at[e, mid + k], land.at[e, there], fwd_send.at[e, there], fwd_recv.at[e, there], index).wait_send()

        for r in range(reach):
            for when, here in ((has_up, mid - 1 - r), (has_down, mid + group + r)):

                @pl.when(when)
                def _():
                    copy(land.at[e, here], land.at[e, here], fwd_send.at[e, here], fwd_recv.at[e, here], me).wait_recv()

    def gather_in(e, reach):
        for k in range(group):
            in_wait(e, k)
            forward_start(e, k, reach)

    def turn(e, dst):
        tiles = land.shape[3] // LANES
        for t in range(tiles):
            x = land[e, :, :, t * LANES : (t + 1) * LANES].reshape(LANES, LANES).T
            low = off + (t - 1) * LANES
            cut = max(0, off - side - low)
            stop = min(LANES, off + own + side - low)
            dst[low + cut : low + stop, :] = x[cut:stop, :]

    def clear_sides(ref):
        @pl.when(first)
        def _():
            ref[off - side : off, :] = jnp.zeros((side, LANES), jnp.float32)

        @pl.when(last)
        def _():
            ref[off + own : off + own + side, :] = jnp.zeros((side, LANES), jnp.float32)

    reach_of = (mid, mid, TILE // band)

    @pl.when(first)
    def _():
        land[:, mid : mid + group, :, 0:LANES] = jnp.zeros((3, group, band, LANES), jnp.float32)

    @pl.when(last)
    def _():
        land[:, mid : mid + group, :, own + LANES :] = jnp.zeros((3, group, band, LANES), jnp.float32)

    @pl.when(jnp.logical_not(has_up))
    def _():
        land[:, 0:mid] = jnp.zeros((3, mid) + land.shape[2:], jnp.float32)
        slots[0:mid] = jnp.full((mid, band, LANES), -1.0, jnp.float32)
        got_up[...] = jnp.zeros_like(got_up)

    @pl.when(jnp.logical_not(has_down))
    def _():
        land[:, mid + group :] = jnp.zeros((3, mid) + land.shape[2:], jnp.float32)
        slots[mid + group :] = jnp.full((mid, band, LANES), -1.0, jnp.float32)
        got_down[...] = jnp.zeros_like(got_down)

    spare = mid - reach_of[2]
    for low in (0, bands - spare):
        land[2, low : low + spare] = jnp.zeros((spare,) + land.shape[2:], jnp.float32)
        slots[low : low + spare] = jnp.full((spare, band, LANES), -1.0, jnp.float32)

    sub = lax.broadcasted_iota(jnp.int32, (band, LANES), 0)
    mine = jnp.zeros((band, LANES), jnp.int32)
    for r in range(band):
        mine = jnp.where(sub == r, slot_of[facet[r]], mine)
    slots[mid + place] = mine.astype(jnp.float32)

    inside = jnp.where(has_up, 1, lane >= margin) * jnp.where(has_down, 1, lane < LANES - margin)
    inside = inside.astype(jnp.float32)
    for k in range(levels):
        d = 2**k
        i = lax.broadcasted_iota(jnp.int32, (2 * LANES, LANES), 0) % LANES
        o = jnp.abs(i - lax.broadcasted_iota(jnp.int32, (2 * LANES, LANES), 1))
        coef = jnp.where(o == 0, 0.375, jnp.where(o == d, 0.25, jnp.where(o == 2 * d, 0.0625, 0.0)))
        cc[k] = (coef * inside).astype(jnp.bfloat16)

    pl.semaphore_wait(barrier, count - 1)

    slot_src = slots.at[mid + place]
    near = reach_of[2]

    def slot_to(fn):
        for j in range(group):

            @pl.when(place != j)
            def _():
                fn(slot_src, slots.at[mid + place], slot_send.at[1, j], slot_recv.at[mid + place], team * group + j)

            @pl.when(has_up & (place < near))
            def _():
                there = mid + group + place
                fn(slot_src, slots.at[there], slot_send.at[0, j], slot_recv.at[there], (team - 1) * group + j)

            @pl.when(has_down & (place >= group - near))
            def _():
                there = mid - group + place
                fn(slot_src, slots.at[there], slot_send.at[2, j], slot_recv.at[there], (team + 1) * group + j)

    slot_to(lambda *a: copy(*a).start())
    share(psf, psf_all, psf_send, psf_recv)
    in_start(1)
    in_start(2)
    in_start(0)
    psf_all[me] = psf[...]
    gather_in(1, reach_of[1])
    collect(psf, psf_all, psf_send, psf_recv)
    slot_to(lambda *a: copy(*a).wait_send())
    for b in range(mid - near, mid + group + near):
        other = has_up if b < mid else has_down if b >= mid + group else place != b - mid

        @pl.when(other)
        def _():
            copy(slots.at[b], slots.at[b], slot_send.at[1, 0], slot_recv.at[b], me).wait_recv()

    rows_slot = slots[...].reshape(LANES, LANES)

    def pick(s, acc):
        tile = psf_all[s]
        hit = rows_slot == s.astype(jnp.float32)
        return tuple(jnp.where(hit, tile[:, h * LANES : (h + 1) * LANES], acc[h]) for h in range(2))

    zero = jnp.zeros((LANES, LANES), jnp.float32)
    taps = jnp.concatenate(lax.fori_loop(0, count, pick, (zero, zero)), axis=1)
    i = lax.broadcasted_iota(jnp.int32, (TILE * TILE, TILE * TILE), 0)
    j = lax.broadcasted_iota(jnp.int32, (TILE * TILE, TILE * TILE), 1)
    swap = ((i // TILE == j % TILE) & (i % TILE == j // TILE)).astype(jnp.float32).astype(jnp.bfloat16)
    high, low = halves(taps)
    taps = dot(high, swap) + dot(low, swap)
    i = lax.broadcasted_iota(jnp.int32, (LANES, LANES), 0)
    j = lax.broadcasted_iota(jnp.int32, (LANES, LANES), 1)
    tap = j - i + HALF
    banded = (tap >= 0) & (tap < TILE)
    per = LANES // TILE
    for h in range(TILE // per):
        skew = pltpu.roll(taps[:, h * LANES : (h + 1) * LANES], LANES - HALF, 1, stride=1, stride_axis=0)
        for n in range(per):
            b = h * per + n
            x = jnp.where(banded, pltpu.roll(skew, LANES - TILE * n, 1) if n else skew, 0.0)
            high, low = halves(x)
            rows = slice(b // SHIFTS * LANES, (b // SHIFTS + 1) * LANES)
            cols = slice(b % SHIFTS * LANES, (b % SHIFTS + 1) * LANES)
            sh[rows, cols] = high
            sl[rows, cols] = low

    forward_done(1, reach_of[1])
    turn(1, tg)

    def multiply(src, low, high, step, table):
        size = block(high - low, 320, 16)

        def one(start):
            x = jnp.concatenate([src[pl.ds(start + low + off + step * n, size), :] for n in range(SHIFTS)], axis=1)
            a, b = halves(x)
            total = table(a, sh[...]) + table(b, sh[...]) + table(a, sl[...])
            for n in range(SHIFTS):
                y[n, pl.ds(start, size), :] = total[:, n * LANES : (n + 1) * LANES]

        over(0, high - low, size, one)

    def added(start, size, shifts):
        total = None
        for n in range(SHIFTS):
            part = y[n, pl.ds(start + shifts[n], size), :]
            total = part if total is None else total + part
        return total

    def blurred(src, low, high, body):
        multiply(src, low - HALF, high + HALF, 1, dot_t)
        size = block(high - low, 256, 8)
        over(low, high, size, lambda c: body(c, size, added(c - low, size, [SHIFTS * n for n in range(SHIFTS)])))

    def adjoint(src, low, high, body):
        multiply(src, low, high + TILE, -SHIFTS, dot)
        size = block(high - low, 256, 8)
        over(low, high, size, lambda c: body(c, size, added(c - low, size, [HALF - n for n in range(SHIFTS)])))

    def step_of(sweep, descent, between):
        back[0:2, :, 0:LANES] = jnp.zeros((2, band, LANES), jnp.float32)

        def tally(c, size, b):
            d = descent[pl.ds(c + off, size), :]
            w = th[pl.ds(c + off, size), :]
            one = (d * d).reshape(size // 8, 8, LANES).sum(axis=0)
            two = (w * b * b).reshape(size // 8, 8, LANES).sum(axis=0)
            back[0, :, 0:LANES] += one
            back[1, :, 0:LANES] += two

        blurred(descent, 0, own, tally)
        keep_rows = (lane >= margin) & (lane < LANES - margin)

        def total(x):
            return jnp.where(keep_rows, jnp.sum(x, axis=0, keepdims=True), 0.0)

        sums[sweep, me] = jnp.concatenate([total(back[0, :, 0:LANES]), total(back[1, :, 0:LANES])], axis=0)
        mine = sums.at[sweep, me]
        share(mine, sums.at[sweep], sum_send.at[sweep], sum_recv.at[sweep])
        between()
        collect(mine, sums.at[sweep], sum_send.at[sweep], sum_recv.at[sweep])
        totals = jnp.sum(jnp.sum(sums[sweep], axis=0), axis=1, keepdims=True)
        return totals[0:1] / totals[1:2]

    def starlet(step, reach, inner, store):
        low, high = off - reach, off + own + reach
        size = block(high - low, 320, 8)
        for k in range(levels):
            d = 2**k
            src, dst = smooth.at[k], smooth.at[k + 1]

            def one(s):
                def at(n):
                    return src[pl.ds(s + n, size), :]

                x = 0.0625 * (at(-2 * d) + at(2 * d)) + 0.25 * (at(-d) + at(d)) + 0.375 * at(0)
                dst[pl.ds(s, size), :] = dot(jnp.concatenate(halves(x), axis=1), cc[k])

            over(low, high, size, one)
            clear_sides(dst)
        limits = [step * thresholds[k] for k in range(levels)]
        low, high = off - inner, off + own + inner
        size = block(high - low, 256, 8)

        def last_pass(s):
            before = smooth[0, pl.ds(s, size), :]
            total = None
            for k in range(levels):
                after = smooth[k + 1, pl.ds(s, size), :]
                detail = before - after
                part = detail - jnp.clip(detail, -limits[k], limits[k])
                total = part if total is None else total + part
                before = after
            store(s, size, total + before)

        over(low, high, size, last_pass)

    def halo_args(n, size):
        return (
            (has_up, pack_up.at[0:size], got_down.at[n, 0:size], halo_send.at[n, 0], halo_recv.at[n, 1], me - group),
            (has_down, pack_down.at[0:size], got_up.at[n, 0:size], halo_send.at[n, 1], halo_recv.at[n, 0], me + group),
        )

    def halo_start(n, ref, inner):
        size = (own + 2 * inner) // (LANES // margin)
        for k in range(LANES // margin):
            x = ref[off - inner + k * size : off - inner + (k + 1) * size, :]
            here = (lane >= k * margin) & (lane < (k + 1) * margin)
            for pack, source in ((pack_up, margin), (pack_down, LANES - 2 * margin)):
                moved = pltpu.roll(x, (k * margin - source) % LANES, 1)
                pack[0:size, :] = moved if k == 0 else jnp.where(here, moved, pack[0:size, :])
        for when, src, dst, send, recv, index in halo_args(n, size):

            @pl.when(when)
            def _():
                copy(src, dst, send, recv, index).start()

    def halo_done(n, inner):
        size = (own + 2 * inner) // (LANES // margin)
        for (when, src, dst, send, recv, index), got, r in zip(halo_args(n, size), (got_up, got_down), (0, 1)):

            @pl.when(when)
            def _():
                copy(src, dst, send, recv, index).wait_send()
                here = got.at[n, 0:size]
                copy(here, here, send, halo_recv.at[n, r], index).wait_recv()

    def with_halo(n, ref, inner):
        size = (own + 2 * inner) // (LANES // margin)
        for k in range(LANES // margin):
            rows = slice(off - inner + k * size, off - inner + (k + 1) * size)
            above = pltpu.roll(got_up[n, 0:size, :], (-k * margin) % LANES, 1)
            below = pltpu.roll(got_down[n, 0:size, :], (LANES - margin - k * margin) % LANES, 1)
            x = jnp.where(lane < margin, above, jnp.where(lane >= LANES - margin, below, ref[rows, :]))
            ref[rows, :] = x

    gather_in(2, reach_of[2])
    forward_done(2, reach_of[2])
    turn(2, th)

    def fetch_image():
        gather_in(0, reach_of[0])
        forward_done(0, reach_of[0])
        turn(0, ti)

    step = step_of(0, tg, fetch_image)

    def trial(step, start, descent, reach):
        low, high = off - reach, off + own + reach

        def one(s):
            smooth[0, pl.ds(s, block(high - low, 256, 8)), :] = (
                start[pl.ds(s, block(high - low, 256, 8)), :] - step * descent[pl.ds(s, block(high - low, 256, 8)), :]
            )

        over(low, high, block(high - low, 256, 8), one)

    trial(step, ti, tg, side)
    inner = margin + TILE

    def store_current(s, size, x):
        cur[pl.ds(s, size), :] = x

    starlet(step, side, inner, store_current)

    halo_start(0, cur, inner)
    halo_done(0, inner)
    with_halo(0, cur, inner)

    def change(s):
        size = block(own + 2 * inner, 256, 8)
        work[pl.ds(s, size), :] = cur[pl.ds(s, size), :] - ti[pl.ds(s, size), :]

    over(off - inner, off + own + inner, block(own + 2 * inner, 256, 8), change)

    def push(c, size, b):
        smooth[0, pl.ds(c + off, size), :] = th[pl.ds(c + off, size), :] * b

    blurred(work, -inner + HALF, own + inner - HALF, push)

    def descend(c, size, b):
        work[pl.ds(c + off, size), :] = (tg[pl.ds(c + off, size), :] + b) * inside

    adjoint(smooth.at[0], -margin, own + margin, descend)
    clear_sides(work)
    halo_start(1, work, margin)
    step = step_of(1, work, lambda: halo_done(1, margin))
    with_halo(1, work, margin)
    trial(step, cur, work, margin)

    def store_back(s, size, x):
        cur[pl.ds(s, size), :] = x

    starlet(step, margin, 0, store_back)
    for t in range(own // LANES):
        x = cur[off + t * LANES : off + (t + 1) * LANES, :].T
        back[:, :, t * LANES : (t + 1) * LANES] = x[margin : LANES - margin].reshape(group, band, LANES)

    def slab(p):
        return out.at[:, pl.ds(pl.multiple_of(p * own, LANES), own)]

    for j in range(group):

        @pl.when(place != j)
        def _():
            copy(back.at[j], slab(place), out_send.at[j], out_recv.at[place], team * group + j).start()

        @pl.when(place == j)
        def _():
            pltpu.make_async_copy(back.at[j], slab(place), out_recv.at[j]).start()

    for e in range(3):
        in_done(e)
    for j in range(group):

        @pl.when(place != j)
        def _():
            copy(back.at[j], slab(place), out_send.at[j], out_recv.at[place], team * group + j).wait_send()

        copy(back.at[j], slab(j), out_send.at[j], out_recv.at[j], me).wait_recv()


def body(image_now, gradient, hessian_weight, psf_tiles, facet_of_row, tile_slot, thresholds):
    band, columns = image_now.shape
    levels = thresholds.shape[0]
    scales = lax.axis_size("scales")
    count = lax.axis_size("rows") * scales
    margin = up8(2 ** (levels + 1) - 2)
    group = (LANES - 2 * margin) // band
    own = columns // group
    teams = count // group
    side = margin + (SUBITERS - 1) * (margin + TILE)
    rows = own + 2 * side + 2 * margin
    bands = LANES // band
    f32 = lambda *shape: pltpu.VMEM(shape, jnp.float32)
    bf16 = lambda *shape: pltpu.VMEM(shape, jnp.bfloat16)
    sem = lambda *shape: pltpu.SemaphoreType.DMA(shape)
    smem = pl.BlockSpec(memory_space=pltpu.SMEM)
    plane = (rows, LANES)
    wide = SHIFTS * LANES
    halo = (own + 2 * (margin + TILE)) // (LANES // margin)
    return pl.pallas_call(
        functools.partial(kernel, count, scales, group, levels, margin),
        out_shape=jax.ShapeDtypeStruct((band, columns), jnp.float32),
        in_specs=[VMEM] * 4 + [smem] * 3,
        out_specs=VMEM,
        scratch_shapes=[
            f32(3, bands, band, own + 2 * LANES), f32(count, 1, TILE * TILE), f32(bands, band, LANES),
            f32(*plane), f32(*plane), f32(*plane), f32(*plane), f32(*plane), f32(levels + 1, *plane),
            f32(SHIFTS, *plane), bf16(wide, wide), bf16(wide, wide), bf16(levels, 2 * LANES, LANES),
            f32(SUBITERS, count, 2, LANES), f32(halo, LANES), f32(halo, LANES), f32(SUBITERS, halo, LANES),
            f32(SUBITERS, halo, LANES), f32(group, band, own),
            sem(count), sem(count), sem(3, group), sem(bands), sem(3, group), sem(3, group),
            sem(3, bands), sem(3, bands), sem(SUBITERS, count), sem(SUBITERS, count),
            sem(SUBITERS, 2), sem(SUBITERS, 2), sem(group), sem(group),
        ],
        compiler_params=pltpu.CompilerParams(
            collective_id=0, has_side_effects=True, vmem_limit_bytes=56 * 1024 * 1024
        ),
    )(image_now, gradient, hessian_weight, psf_tiles, facet_of_row, tile_slot, thresholds)


def solution(mesh):
    band = P(AXES, None)
    in_specs = (band, band, band, band, P(AXES), P(), P())
    return jax.shard_map(body, mesh=mesh, in_specs=in_specs, out_specs=band, check_vma=False)
```

time: 122 us -> 80.3 us (0.66)
  Pallas kernels: 118 us -> 77.7 us
  other arithmetic: 1.26 us -> 0 us
    pallas_call x1, Pallas kernels: 118 us -> 77.7 us  [body(): pl.pallas_call(functools.partial(kernel, count, scales, group, levels, ma...]
where the time goes in v1:
time: 80.3 us; the launch traced here: 79.4 us
  Pallas kernels  77.7 us (97%)
  local copies, waits for them, and re-layouts  1.67 us (2%)
    pallas_call x1, Pallas kernels, body(): pl.pallas_call(functools.partial(kernel, count, scales, group, levels, ma...  77.7 us
    unnamed x1, local copies, waits for them, and re-layouts  1.67 us

profile of v1, /device:TPU:13, one launch (start us, length us, event | category | flops | bytes accessed | tf_op | source)
XLA Modules:
  0.0 79.4 jit_solution(16248702803282300114)
XLA Ops:
  0.0 77.7 %shard_map.73 = f32[8,8192]{1,0:T(8,128)} custom-call(f32[8,8192]{1,0:T(8,128)} %image.1, f32[8,8192]{1,0:T(8,128)} %gradient.1, f32[8,8192]{1,0:T(8,128)} %weight.1, f32[1,256]{1,0:T(1,128)} %psf.1, s32[8]{0:T(128)} %facet.1, s32[32]{0:T(128)} %slot_of.1, f32[4]{0:T(128)} %thresholds.1), custom_call_target="tpu_custom_call" | custom-call | tf_op jit(solution)/shard_map/pallas_call | solution.py:543
  77.7 1.7 %copy.9 = f32[8,8192]{1,0:T(8,128)} copy(f32[8,8192]{1,0:T(8,128)} %shard_map.73) | data formatting | bytes 524288
